TPU v7x, 32 devices: a whole 2x2x4 slice. The times are simulated.
32 devices in a mesh: ka: 16 (over z, x, core), ga: 2 (over y).
Axes of the slice: x: 2, y: 2, z: 4, core: 2. Of those that a mesh axis runs over, the one named last changes fastest.
Arguments:
- pair_density: bfloat16 [256, 64, 4096], P('ka', None, 'ga'), may hold values from -0.1875 to 0.1875
- trial_vectors: bfloat16 [256, 64, 128], P('ka'), may hold values from -6 to 6
- energy: float32 [256, 64], P('ka'), may hold values from 0.5 to 2.5
- coulomb: float32 [4096], P('ga'), may hold values from 0.03 to 0.3
- screen: bfloat16 [32, 4096, 256], P(None, 'ga'), may hold values from -0.375 to 0.375
- neighbors: int32 [256, 16], P('ka'), may hold values from 0 to 255, as said below
- live_count: int32 [256], P('ka'), may hold values from 1 to 16, as said below
- q_index: int32 [256, 16], P('ka'), may hold values from 0 to 31
Outputs:
- applied: bfloat16 [256, 64, 128], P('ka', 'ga')
Inputs may be any that keep to these rules, and one draw needn't show every extreme that they name: `neighbors`: the 16 partners of k-point k are distinct k-points whose block k' // 16 is the block of k or one of its two neighbours on the closed cycle of 16 blocks. Only the first live_count[k] slots of row k of neighbors and q_index are used; some k-point uses all 16.
All inputs are finite; a program needn't handle non-finite values.
Results may differ from a plain program's by a relative error of at most 0.013.
Values may be sent and summed in bfloat16 or wider, within the bound.
No kernel may reach another device: no remote copies, remote signals or barrier semaphores. Data moves between devices by JAX's collectives and lax.ppermute only.
A program may use at most 192 MiB of HBM per device.

v0:
```python
import jax
import jax.numpy as jnp
from jax import lax
from jax.sharding import PartitionSpec as P


def passed_along(value, axis, steps):
    count = lax.axis_size(axis)
    pairs = [(source, (source + steps) % count) for source in range(count)]
    return lax.ppermute(value, axis, pairs)


def form_products(density, vectors):
    return jnp.einsum("kpg,kpt->kgt", density, vectors, preferred_element_type=jnp.float32).astype(
        jnp.bfloat16
    )


def on_device(pair_density, trial_vectors, energy, coulomb, screen, neighbors, live_count, q_index):
    local_k, pair_count, local_g = pair_density.shape
    trial_count = trial_vectors.shape[2]
    block_size = screen.shape[2]
    groups = local_g // block_size
    cycle_size = lax.axis_size("ka")
    position = lax.axis_index("ka")
    own_products = form_products(pair_density, trial_vectors)
    below_block = passed_along(own_products, "ka", 1)
    above_block = passed_along(own_products, "ka", -1)
    window = jnp.concatenate([below_block, own_products, above_block], axis=0)
    partial_value = jnp.sum(own_products, axis=0, dtype=jnp.float32)
    density_total = lax.psum(partial_value, "ka")
    screened = coulomb[:, None] * density_total
    offset = (neighbors // local_k - position + 1) % cycle_size
    local_index = offset * local_k + neighbors % local_k

    def add_slot(slot_index, summed):
        picked = jnp.take(window, local_index[:, slot_index], axis=0)
        blocks = jnp.take(screen, q_index[:, slot_index], axis=0)
        coupled = jnp.einsum(
            "kbgc,kbct->kbgt",
            blocks.reshape(local_k, groups, block_size, block_size),
            picked.reshape(local_k, groups, block_size, trial_count),
            preferred_element_type=jnp.float32,
        ).reshape(local_k, local_g, trial_count)
        is_live = (slot_index < live_count)[:, None, None]
        return summed + jnp.where(is_live, coupled, 0.0)

    last_slot = neighbors.shape[1]
    direct = lax.fori_loop(
        0, last_slot, add_slot, jnp.zeros((local_k, local_g, trial_count), jnp.float32)
    )
    kernel = (2.0 * screened[None] - direct).astype(jnp.bfloat16)
    pair_terms = jnp.einsum(
        "kpg,kgt->kpt", pair_density, kernel, preferred_element_type=jnp.float32
    )
    mine = lax.psum_scatter(pair_terms, "ga", scatter_dimension=1, tiled=True)
    row_count = mine.shape[1]
    first_row = lax.axis_index("ga") * row_count
    energy_rows = lax.dynamic_slice_in_dim(energy, first_row, row_count, 1)
    vector_rows = lax.dynamic_slice_in_dim(trial_vectors, first_row, row_count, 1)
    return (energy_rows[:, :, None] * vector_rows.astype(jnp.float32) + mine).astype(jnp.bfloat16)


def solution(mesh):
    in_specs = (
        P("ka", None, "ga"),
        P("ka", None, None),
        P("ka", None),
        P("ga"),
        P(None, "ga", None),
        P("ka", None),
        P("ka"),
        P("ka", None),
    )
    out_specs = P("ka", "ga", None)
    return jax.shard_map(
        on_device, mesh=mesh, in_specs=in_specs, out_specs=out_specs, check_vma=False
    )
```

profile of v0, /device:TPU:0, one launch (start us, length us, event | category | flops | bytes accessed | tf_op | source)
XLA Modules:
  0.0 1172.0 jit_solution(3300030302084759185)
XLA Ops:
  23.2 165.4 %all-reduce.2.cloned.1.call-done = f32[2048,128]{1,0:T(8,128)} async-done(((f32[2048,128]{1,0:T(8,128)}), f32[2048,128]{1,0:T(8,128)}) %all-reduce.2.cloned.1.call-update) | async-done | bytes 1048592 | tf_op jit(solution)/shard_map/psum | solution.py:31
  191.1 17.6 %pad_maximum_fusion = bf16[48,2048,128]{2,1,0:T(8,128)(2,1)} fusion(bf16[16,2048,128]{2,1,0:T(8,128)(2,1)} %collective-permute-done.1, bf16[16,2048,128]{2,1,0:T(8,128)(2,1)} %get-tuple-element.182, bf16[16,2048,128]{2,1,0:T(8,128)(2,1)} %collective-permute-done), kind=kLoop, calls=%fused_computation.19 | loop fusion | flops 25165824 | bytes 50331648 | tf_op jit(solution)/shard_map/concatenate | solution.py:29
  208.7 909.0 %while.14 = (s32[]{:T(128)}, f32[16,2048,128]{2,1,0:T(8,128)}, s32[16]{0:T(128)S(1)}, s32[16,16]{0,1:T(8,128)S(1)}, bf16[32,2048,256]{2,1,0:T(8,128)(2,1)}, /*in...) while((s32[]{:T(128)}, f32[16,2048,128]{2,1,0:T(8,128)}, ...), condition=%wide.region_3.4_spmd.clone, body=%wide.region_2.3_spmd.clone.sunk | while | flops 2172651776 | bytes 142615312 | solution.py:49
  233.5 14.0 %fusion.27 = f32[16,8,256,128]{3,2,1,0:T(8,128)} fusion(bf16[16,8,256,256]{3,2,1,0:T(8,128)(2,1)} %bitcast.29, pred[16]{0:T(512)(128)(4,1)S(1)} %get-tuple-element.231, bf16[16,8,256,128]{3,2,1,0:T(8,128)(2,1)} %bitcast.30, pred[16]{0:T(512)(128)(4,1)S(1)} %get-tuple-element.233), kind=kOutput, calls=%fused_computation.4.clone.1 | convolution fusion | flops 2160066560 | bytes 41943072 | tf_op jit(solution)/shard_map/while/body/eval_jaxpr/kbgc,kbct->kbgt/dot_general | solution.py:39
  299.3 17.8 %fusion.28 = f32[16,2048,128]{2,1,0:T(8,128)} fusion(f32[16,8,256,128]{3,2,1,0:T(8,128)} %fusion.27, f32[16,2048,128]{2,1,0:T(8,128)} %get-tuple-element.244, pred[16]{0:T(512)(128)(4,1)S(1)} %broadcast_compare_fusion.2, pred[]{:T(512)S(6)} %compare.7), kind=kLoop, calls=%fused_computation.3.clone.1 | loop fusion | flops 12582912 | bytes 50331664 | tf_op jit(solution)/shard_map/while/body/eval_jaxpr/add | solution.py:46
  342.0 14.0 %fusion.27 = f32[16,8,256,128]{3,2,1,0:T(8,128)} fusion(bf16[16,8,256,256]{3,2,1,0:T(8,128)(2,1)} %bitcast.29, pred[16]{0:T(512)(128)(4,1)S(1)} %get-tuple-element.231, bf16[16,8,256,128]{3,2,1,0:T(8,128)(2,1)} %bitcast.30, pred[16]{0:T(512)(128)(4,1)S(1)} %get-tuple-element.233), kind=kOutput, calls=%fused_computation.4.clone.1 | convolution fusion | flops 2160066560 | bytes 41943072 | tf_op jit(solution)/shard_map/while/body/eval_jaxpr/kbgc,kbct->kbgt/dot_general | solution.py:39
  356.0 17.8 %fusion.28 = f32[16,2048,128]{2,1,0:T(8,128)} fusion(f32[16,8,256,128]{3,2,1,0:T(8,128)} %fusion.27, f32[16,2048,128]{2,1,0:T(8,128)} %get-tuple-element.244, pred[16]{0:T(512)(128)(4,1)S(1)} %broadcast_compare_fusion.2, pred[]{:T(512)S(6)} %compare.7), kind=kLoop, calls=%fused_computation.3.clone.1 | loop fusion | flops 12582912 | bytes 50331664 | tf_op jit(solution)/shard_map/while/body/eval_jaxpr/add | solution.py:46
  398.9 14.0 %fusion.27 = f32[16,8,256,128]{3,2,1,0:T(8,128)} fusion(bf16[16,8,256,256]{3,2,1,0:T(8,128)(2,1)} %bitcast.29, pred[16]{0:T(512)(128)(4,1)S(1)} %get-tuple-element.231, bf16[16,8,256,128]{3,2,1,0:T(8,128)(2,1)} %bitcast.30, pred[16]{0:T(512)(128)(4,1)S(1)} %get-tuple-element.233), kind=kOutput, calls=%fused_computation.4.clone.1 | convolution fusion | flops 2160066560 | bytes 41943072 | tf_op jit(solution)/shard_map/while/body/eval_jaxpr/kbgc,kbct->kbgt/dot_general | solution.py:39
  413.0 17.8 %fusion.28 = f32[16,2048,128]{2,1,0:T(8,128)} fusion(f32[16,8,256,128]{3,2,1,0:T(8,128)} %fusion.27, f32[16,2048,128]{2,1,0:T(8,128)} %get-tuple-element.244, pred[16]{0:T(512)(128)(4,1)S(1)} %broadcast_compare_fusion.2, pred[]{:T(512)S(6)} %compare.7), kind=kLoop, calls=%fused_computation.3.clone.1 | loop fusion | flops 12582912 | bytes 50331664 | tf_op jit(solution)/shard_map/while/body/eval_jaxpr/add | solution.py:46
  455.6 14.0 %fusion.27 = f32[16,8,256,128]{3,2,1,0:T(8,128)} fusion(bf16[16,8,256,256]{3,2,1,0:T(8,128)(2,1)} %bitcast.29, pred[16]{0:T(512)(128)(4,1)S(1)} %get-tuple-element.231, bf16[16,8,256,128]{3,2,1,0:T(8,128)(2,1)} %bitcast.30, pred[16]{0:T(512)(128)(4,1)S(1)} %get-tuple-element.233), kind=kOutput, calls=%fused_computation.4.clone.1 | convolution fusion | flops 2160066560 | bytes 41943072 | tf_op jit(solution)/shard_map/while/body/eval_jaxpr/kbgc,kbct->kbgt/dot_general | solution.py:39
  469.6 17.8 %fusion.28 = f32[16,2048,128]{2,1,0:T(8,128)} fusion(f32[16,8,256,128]{3,2,1,0:T(8,128)} %fusion.27, f32[16,2048,128]{2,1,0:T(8,128)} %get-tuple-element.244, pred[16]{0:T(512)(128)(4,1)S(1)} %broadcast_compare_fusion.2, pred[]{:T(512)S(6)} %compare.7), kind=kLoop, calls=%fused_computation.3.clone.1 | loop fusion | flops 12582912 | bytes 50331664 | tf_op jit(solution)/shard_map/while/body/eval_jaxpr/add | solution.py:46
  512.3 14.0 %fusion.27 = f32[16,8,256,128]{3,2,1,0:T(8,128)} fusion(bf16[16,8,256,256]{3,2,1,0:T(8,128)(2,1)} %bitcast.29, pred[16]{0:T(512)(128)(4,1)S(1)} %get-tuple-element.231, bf16[16,8,256,128]{3,2,1,0:T(8,128)(2,1)} %bitcast.30, pred[16]{0:T(512)(128)(4,1)S(1)} %get-tuple-element.233), kind=kOutput, calls=%fused_computation.4.clone.1 | convolution fusion | flops 2160066560 | bytes 41943072 | tf_op jit(solution)/shard_map/while/body/eval_jaxpr/kbgc,kbct->kbgt/dot_general | solution.py:39
  526.3 17.8 %fusion.28 = f32[16,2048,128]{2,1,0:T(8,128)} fusion(f32[16,8,256,128]{3,2,1,0:T(8,128)} %fusion.27, f32[16,2048,128]{2,1,0:T(8,128)} %get-tuple-element.244, pred[16]{0:T(512)(128)(4,1)S(1)} %broadcast_compare_fusion.2, pred[]{:T(512)S(6)} %compare.7), kind=kLoop, calls=%fused_computation.3.clone.1 | loop fusion | flops 12582912 | bytes 50331664 | tf_op jit(solution)/shard_map/while/body/eval_jaxpr/add | solution.py:46
  583.1 17.8 %fusion.28 = f32[16,2048,128]{2,1,0:T(8,128)} fusion(f32[16,8,256,128]{3,2,1,0:T(8,128)} %fusion.27, f32[16,2048,128]{2,1,0:T(8,128)} %get-tuple-element.244, pred[16]{0:T(512)(128)(4,1)S(1)} %broadcast_compare_fusion.2, pred[]{:T(512)S(6)} %compare.7), kind=kLoop, calls=%fused_computation.3.clone.1 | loop fusion | flops 12582912 | bytes 50331664 | tf_op jit(solution)/shard_map/while/body/eval_jaxpr/add | solution.py:46
  626.3 14.0 %fusion.27 = f32[16,8,256,128]{3,2,1,0:T(8,128)} fusion(bf16[16,8,256,256]{3,2,1,0:T(8,128)(2,1)} %bitcast.29, pred[16]{0:T(512)(128)(4,1)S(1)} %get-tuple-element.231, bf16[16,8,256,128]{3,2,1,0:T(8,128)(2,1)} %bitcast.30, pred[16]{0:T(512)(128)(4,1)S(1)} %get-tuple-element.233), kind=kOutput, calls=%fused_computation.4.clone.1 | convolution fusion | flops 2160066560 | bytes 41943072 | tf_op jit(solution)/shard_map/while/body/eval_jaxpr/kbgc,kbct->kbgt/dot_general | solution.py:39
  640.4 17.8 %fusion.28 = f32[16,2048,128]{2,1,0:T(8,128)} fusion(f32[16,8,256,128]{3,2,1,0:T(8,128)} %fusion.27, f32[16,2048,128]{2,1,0:T(8,128)} %get-tuple-element.244, pred[16]{0:T(512)(128)(4,1)S(1)} %broadcast_compare_fusion.2, pred[]{:T(512)S(6)} %compare.7), kind=kLoop, calls=%fused_computation.3.clone.1 | loop fusion | flops 12582912 | bytes 50331664 | tf_op jit(solution)/shard_map/while/body/eval_jaxpr/add | solution.py:46
  697.0 17.8 %fusion.28 = f32[16,2048,128]{2,1,0:T(8,128)} fusion(f32[16,8,256,128]{3,2,1,0:T(8,128)} %fusion.27, f32[16,2048,128]{2,1,0:T(8,128)} %get-tuple-element.244, pred[16]{0:T(512)(128)(4,1)S(1)} %broadcast_compare_fusion.2, pred[]{:T(512)S(6)} %compare.7), kind=kLoop, calls=%fused_computation.3.clone.1 | loop fusion | flops 12582912 | bytes 50331664 | tf_op jit(solution)/shard_map/while/body/eval_jaxpr/add | solution.py:46
  739.7 14.0 %fusion.27 = f32[16,8,256,128]{3,2,1,0:T(8,128)} fusion(bf16[16,8,256,256]{3,2,1,0:T(8,128)(2,1)} %bitcast.29, pred[16]{0:T(512)(128)(4,1)S(1)} %get-tuple-element.231, bf16[16,8,256,128]{3,2,1,0:T(8,128)(2,1)} %bitcast.30, pred[16]{0:T(512)(128)(4,1)S(1)} %get-tuple-element.233), kind=kOutput, calls=%fused_computation.4.clone.1 | convolution fusion | flops 2160066560 | bytes 41943072 | tf_op jit(solution)/shard_map/while/body/eval_jaxpr/kbgc,kbct->kbgt/dot_general | solution.py:39
  753.7 17.8 %fusion.28 = f32[16,2048,128]{2,1,0:T(8,128)} fusion(f32[16,8,256,128]{3,2,1,0:T(8,128)} %fusion.27, f32[16,2048,128]{2,1,0:T(8,128)} %get-tuple-element.244, pred[16]{0:T(512)(128)(4,1)S(1)} %broadcast_compare_fusion.2, pred[]{:T(512)S(6)} %compare.7), kind=kLoop, calls=%fused_computation.3.clone.1 | loop fusion | flops 12582912 | bytes 50331664 | tf_op jit(solution)/shard_map/while/body/eval_jaxpr/add | solution.py:46
  796.4 14.0 %fusion.27 = f32[16,8,256,128]{3,2,1,0:T(8,128)} fusion(bf16[16,8,256,256]{3,2,1,0:T(8,128)(2,1)} %bitcast.29, pred[16]{0:T(512)(128)(4,1)S(1)} %get-tuple-element.231, bf16[16,8,256,128]{3,2,1,0:T(8,128)(2,1)} %bitcast.30, pred[16]{0:T(512)(128)(4,1)S(1)} %get-tuple-element.233), kind=kOutput, calls=%fused_computation.4.clone.1 | convolution fusion | flops 2160066560 | bytes 41943072 | tf_op jit(solution)/shard_map/while/body/eval_jaxpr/kbgc,kbct->kbgt/dot_general | solution.py:39
  810.4 17.8 %fusion.28 = f32[16,2048,128]{2,1,0:T(8,128)} fusion(f32[16,8,256,128]{3,2,1,0:T(8,128)} %fusion.27, f32[16,2048,128]{2,1,0:T(8,128)} %get-tuple-element.244, pred[16]{0:T(512)(128)(4,1)S(1)} %broadcast_compare_fusion.2, pred[]{:T(512)S(6)} %compare.7), kind=kLoop, calls=%fused_computation.3.clone.1 | loop fusion | flops 12582912 | bytes 50331664 | tf_op jit(solution)/shard_map/while/body/eval_jaxpr/add | solution.py:46
  854.9 14.0 %fusion.27 = f32[16,8,256,128]{3,2,1,0:T(8,128)} fusion(bf16[16,8,256,256]{3,2,1,0:T(8,128)(2,1)} %bitcast.29, pred[16]{0:T(512)(128)(4,1)S(1)} %get-tuple-element.231, bf16[16,8,256,128]{3,2,1,0:T(8,128)(2,1)} %bitcast.30, pred[16]{0:T(512)(128)(4,1)S(1)} %get-tuple-element.233), kind=kOutput, calls=%fused_computation.4.clone.1 | convolution fusion | flops 2160066560 | bytes 41943072 | tf_op jit(solution)/shard_map/while/body/eval_jaxpr/kbgc,kbct->kbgt/dot_general | solution.py:39
  868.9 17.8 %fusion.28 = f32[16,2048,128]{2,1,0:T(8,128)} fusion(f32[16,8,256,128]{3,2,1,0:T(8,128)} %fusion.27, f32[16,2048,128]{2,1,0:T(8,128)} %get-tuple-element.244, pred[16]{0:T(512)(128)(4,1)S(1)} %broadcast_compare_fusion.2, pred[]{:T(512)S(6)} %compare.7), kind=kLoop, calls=%fused_computation.3.clone.1 | loop fusion | flops 12582912 | bytes 50331664 | tf_op jit(solution)/shard_map/while/body/eval_jaxpr/add | solution.py:46
  913.3 14.0 %fusion.27 = f32[16,8,256,128]{3,2,1,0:T(8,128)} fusion(bf16[16,8,256,256]{3,2,1,0:T(8,128)(2,1)} %bitcast.29, pred[16]{0:T(512)(128)(4,1)S(1)} %get-tuple-element.231, bf16[16,8,256,128]{3,2,1,0:T(8,128)(2,1)} %bitcast.30, pred[16]{0:T(512)(128)(4,1)S(1)} %get-tuple-element.233), kind=kOutput, calls=%fused_computation.4.clone.1 | convolution fusion | flops 2160066560 | bytes 41943072 | tf_op jit(solution)/shard_map/while/body/eval_jaxpr/kbgc,kbct->kbgt/dot_general | solution.py:39
  927.3 17.8 %fusion.28 = f32[16,2048,128]{2,1,0:T(8,128)} fusion(f32[16,8,256,128]{3,2,1,0:T(8,128)} %fusion.27, f32[16,2048,128]{2,1,0:T(8,128)} %get-tuple-element.244, pred[16]{0:T(512)(128)(4,1)S(1)} %broadcast_compare_fusion.2, pred[]{:T(512)S(6)} %compare.7), kind=kLoop, calls=%fused_computation.3.clone.1 | loop fusion | flops 12582912 | bytes 50331664 | tf_op jit(solution)/shard_map/while/body/eval_jaxpr/add | solution.py:46
  970.3 14.0 %fusion.27 = f32[16,8,256,128]{3,2,1,0:T(8,128)} fusion(bf16[16,8,256,256]{3,2,1,0:T(8,128)(2,1)} %bitcast.29, pred[16]{0:T(512)(128)(4,1)S(1)} %get-tuple-element.231, bf16[16,8,256,128]{3,2,1,0:T(8,128)(2,1)} %bitcast.30, pred[16]{0:T(512)(128)(4,1)S(1)} %get-tuple-element.233), kind=kOutput, calls=%fused_computation.4.clone.1 | convolution fusion | flops 2160066560 | bytes 41943072 | tf_op jit(solution)/shard_map/while/body/eval_jaxpr/kbgc,kbct->kbgt/dot_general | solution.py:39
  984.4 17.8 %fusion.28 = f32[16,2048,128]{2,1,0:T(8,128)} fusion(f32[16,8,256,128]{3,2,1,0:T(8,128)} %fusion.27, f32[16,2048,128]{2,1,0:T(8,128)} %get-tuple-element.244, pred[16]{0:T(512)(128)(4,1)S(1)} %broadcast_compare_fusion.2, pred[]{:T(512)S(6)} %compare.7), kind=kLoop, calls=%fused_computation.3.clone.1 | loop fusion | flops 12582912 | bytes 50331664 | tf_op jit(solution)/shard_map/while/body/eval_jaxpr/add | solution.py:46
  1028.2 14.0 %fusion.27 = f32[16,8,256,128]{3,2,1,0:T(8,128)} fusion(bf16[16,8,256,256]{3,2,1,0:T(8,128)(2,1)} %bitcast.29, pred[16]{0:T(512)(128)(4,1)S(1)} %get-tuple-element.231, bf16[16,8,256,128]{3,2,1,0:T(8,128)(2,1)} %bitcast.30, pred[16]{0:T(512)(128)(4,1)S(1)} %get-tuple-element.233), kind=kOutput, calls=%fused_computation.4.clone.1 | convolution fusion | flops 2160066560 | bytes 41943072 | tf_op jit(solution)/shard_map/while/body/eval_jaxpr/kbgc,kbct->kbgt/dot_general | solution.py:39
  1042.2 17.8 %fusion.28 = f32[16,2048,128]{2,1,0:T(8,128)} fusion(f32[16,8,256,128]{3,2,1,0:T(8,128)} %fusion.27, f32[16,2048,128]{2,1,0:T(8,128)} %get-tuple-element.244, pred[16]{0:T(512)(128)(4,1)S(1)} %broadcast_compare_fusion.2, pred[]{:T(512)S(6)} %compare.7), kind=kLoop, calls=%fused_computation.3.clone.1 | loop fusion | flops 12582912 | bytes 50331664 | tf_op jit(solution)/shard_map/while/body/eval_jaxpr/add | solution.py:46
  1085.8 14.0 %fusion.27 = f32[16,8,256,128]{3,2,1,0:T(8,128)} fusion(bf16[16,8,256,256]{3,2,1,0:T(8,128)(2,1)} %bitcast.29, pred[16]{0:T(512)(128)(4,1)S(1)} %get-tuple-element.231, bf16[16,8,256,128]{3,2,1,0:T(8,128)(2,1)} %bitcast.30, pred[16]{0:T(512)(128)(4,1)S(1)} %get-tuple-element.233), kind=kOutput, calls=%fused_computation.4.clone.1 | convolution fusion | flops 2160066560 | bytes 41943072 | tf_op jit(solution)/shard_map/while/body/eval_jaxpr/kbgc,kbct->kbgt/dot_general | solution.py:39
  1099.9 17.8 %fusion.28 = f32[16,2048,128]{2,1,0:T(8,128)} fusion(f32[16,8,256,128]{3,2,1,0:T(8,128)} %fusion.27, f32[16,2048,128]{2,1,0:T(8,128)} %get-tuple-element.244, pred[16]{0:T(512)(128)(4,1)S(1)} %broadcast_compare_fusion.2, pred[]{:T(512)S(6)} %compare.7), kind=kLoop, calls=%fused_computation.3.clone.1 | loop fusion | flops 12582912 | bytes 50331664 | tf_op jit(solution)/shard_map/while/body/eval_jaxpr/add | solution.py:46
  1128.9 34.5 %reduce-scatter.2.cloned.1.call-done = f32[16,32,128]{2,1,0:T(8,128)} async-done(((f32[16,64,128]{2,1,0:T(8,128)}), f32[16,32,128]{2,1,0:T(8,128)}) %reduce-scatter.2.cloned.1.call-update) | async-done | bytes 262160 | tf_op jit(solution)/shard_map/reduce_scatter | solution.py:56
  (125 shorter events, 490.9 us)
Async XLA Ops:
  6.5 1122.3 %copy-start = (f32[16,64]{1,0:T(8,128)S(1)}, f32[16,64]{1,0:T(8,128)}, u32[]{:S(2)}) copy-start(f32[16,64]{1,0:T(8,128)} %param.12) | copy-start | bytes 12292
  6.5 182.0 %all-reduce.2.cloned.1.call-start = ((), (), s32[]{:S(2)}) async-start(), calls=%async_computation.1 | async-start | bytes 2097152 | tf_op jit(solution)/shard_map/psum | solution.py:31
  16.1 175.0 %collective-permute-start = (bf16[16,2048,128]{2,1,0:T(8,128)(2,1)}, bf16[16,2048,128]{2,1,0:T(8,128)(2,1)}, u32[]{:S(2)}, u32[]{:S(2)}) collective-permute-start(bf16[16,2048,128]{2,1,0:T(8,128)(2,1)} %get-tuple-element.182), channel_id=1, source_target_pairs={{0,2},{2,4},{4,6},{6,8},{8,10},{10,12},{12,14},{14,16},{16,18},{18... | collective-permute-start | bytes 25165832 | tf_op jit(solution)/shard_map/ppermute | solution.py:10
  16.6 174.5 %collective-permute-start.1 = (bf16[16,2048,128]{2,1,0:T(8,128)(2,1)}, bf16[16,2048,128]{2,1,0:T(8,128)(2,1)}, u32[]{:S(2)}, u32[]{:S(2)}) collective-permute-start(bf16[16,2048,128]{2,1,0:T(8,128)(2,1)} %get-tuple-element.182), channel_id=1, source_target_pairs={{0,30},{2,0},{4,2},{6,4},{8,6},{10,8},{12,10},{14,12},{16,14},{18,... | collective-permute-start | bytes 25165832 | tf_op jit(solution)/shard_map/ppermute | solution.py:10
  21.6 1141.9 %reduce-scatter.2.cloned.1.call-start = ((), (), s32[]{:S(2)}) async-start(), calls=%async_computation.2 | async-start | bytes 786432 | tf_op jit(solution)/shard_map/reduce_scatter | solution.py:56
  191.1 17.6 %copy-start.3 = (s32[16]{0:T(128)S(1)}, s32[16]{0:T(128)}, u32[]{:S(2)}) copy-start(s32[16]{0:T(128)} %param.16) | copy-start | bytes 196
  208.7 909.0 %copy-start.1 = (f32[2048,128]{1,0:T(8,128)S(1)}, f32[2048,128]{1,0:T(8,128)}, u32[]{:S(2)}) copy-start(f32[2048,128]{1,0:T(8,128)} %multiply_multiply_fusion) | copy-start | bytes 3145732
  1117.7 45.7 %copy-start.2 = (bf16[16,64,128]{2,1,0:T(8,128)(2,1)S(1)}, bf16[16,64,128]{2,1,0:T(8,128)(2,1)}, u32[]{:S(2)}) copy-start(bf16[16,64,128]{2,1,0:T(8,128)(2,1)} %param.11) | copy-start | bytes 786436
Sparse Core Ops, SparseCore 0:
  21.7 166.8 all-reduce.1
  1128.9 34.4 reduce-scatter.1
where the time goes:
time: 1170 us
  local copies, waits for them, and re-layouts  406 us (35%)
  other arithmetic  302 us (26%)
  matrix products  245 us (21%)
  waiting for transfers between devices  200 us (17%)
  between operations  13.5 us (1%)
    add x16, other arithmetic, add_slot(): return summed + jnp.where(is_live, coupled, 0.0)  279 us
    dot_general x16, matrix products, add_slot(): jnp.einsum('kbgc,kbct->kbgt', blocks.reshape(local_k, groups, block_size,...  224 us
    gather x16, local copies, waits for them, and re-layouts, add_slot(): picked = jnp.take(window, local_index[:, slot_index], axis=0)  208 us
    gather x16, local copies, waits for them, and re-layouts, add_slot(): blocks = jnp.take(screen, q_index[:, slot_index], axis=0)  197 us
    psum x1, waiting for transfers between devices, on_device(): density_total = lax.psum(partial_value, 'ka')  165 us
    reduce_scatter x1, waiting for transfers between devices, on_device(): mine = lax.psum_scatter(pair_terms, 'ga', scatter_dimension=1, tiled=True)  34.5 us
  transfers between devices with their start and end apart: 4, of which 2 were waited for; matrix products, arithmetic and copies ran while one was open for 0% of the time, Pallas kernels for 0%

commit v1 on v0

--- a/solution.py
+++ b/solution.py
@@ -28,7 +28,7 @@
     above_block = passed_along(own_products, "ka", -1)
     window = jnp.concatenate([below_block, own_products, above_block], axis=0)
     partial_value = jnp.sum(own_products, axis=0, dtype=jnp.float32)
-    density_total = lax.psum(partial_value, "ka")
+    density_total = jnp.sum(lax.all_gather(partial_value, "ka"), axis=0)
     screened = coulomb[:, None] * density_total
     offset = (neighbors // local_k - position + 1) % cycle_size
     local_index = offset * local_k + neighbors % local_k

time: 1170 us -> 1230 us (1.051)
  waiting for transfers between devices: 200 us -> 249 us
    psum x1 -> x0, waiting for transfers between devices: 165 us -> none  [on_device(): density_total = lax.psum(partial_value, 'ka')]
    ppermute x2, waiting for transfers between devices: 0.01 us -> 124 us  [passed_along(): return lax.ppermute(value, axis, pairs)]
    reduce_scatter x1, waiting for transfers between devices: 34.5 us -> 126 us  [on_device(): mine = lax.psum_scatter(pair_terms, 'ga', scatter_dimension=1, tiled=True)]
  transfers between devices with their start and end apart: 4 -> 4, of which waited for: 2 -> 2; matrix products, arithmetic and copies ran while one was open for 0% -> 76% of each run, Pallas kernels for 0% -> 0%
where the time goes in v1:
time: 1230 us
  local copies, waits for them, and re-layouts  407 us (33%)
  other arithmetic  307 us (25%)
  waiting for transfers between devices  249 us (20%)
  matrix products  246 us (20%)
  between operations  13.5 us (1%)
    add x16, other arithmetic, add_slot(): return summed + jnp.where(is_live, coupled, 0.0)  280 us
    dot_general x16, matrix products, add_slot(): jnp.einsum('kbgc,kbct->kbgt', blocks.reshape(local_k, groups, block_size,...  226 us
    gather x16, local copies, waits for them, and re-layouts, add_slot(): picked = jnp.take(window, local_index[:, slot_index], axis=0)  209 us
    gather x16, local copies, waits for them, and re-layouts, add_slot(): blocks = jnp.take(screen, q_index[:, slot_index], axis=0)  197 us
    reduce_scatter x1, waiting for transfers between devices, on_device(): mine = lax.psum_scatter(pair_terms, 'ga', scatter_dimension=1, tiled=True)  126 us
    ppermute x2, waiting for transfers between devices, passed_along(): return lax.ppermute(value, axis, pairs)  124 us
  transfers between devices with their start and end apart: 4, of which 2 were waited for; matrix products, arithmetic and copies ran while one was open for 76% of the time, Pallas kernels for 0%

profile of v1, /device:TPU:0, one launch (start us, length us, event | category | flops | bytes accessed | tf_op | source)
XLA Modules:
  0.0 1228.2 jit_solution(17261426957635453595)
XLA Ops:
  23.2 123.7 %collective-permute-done = bf16[16,2048,128]{2,1,0:T(8,128)(2,1)} collective-permute-done((bf16[16,2048,128]{2,1,0:T(8,128)(2,1)}, bf16[16,2048,128]{2,1,0:T(8,128)(2,1)}, u32[]{:S(2)}, u32[]{:S(2)}) %collective-permute-start) | collective-permute-done | bytes 8388640 | tf_op jit(solution)/shard_map/ppermute | solution.py:10
  146.9 18.5 %pad_maximum_fusion = bf16[48,2048,128]{2,1,0:T(8,128)(2,1)} fusion(bf16[16,2048,128]{2,1,0:T(8,128)(2,1)} %collective-permute-done.1, bf16[16,2048,128]{2,1,0:T(8,128)(2,1)} %get-tuple-element.189, bf16[16,2048,128]{2,1,0:T(8,128)(2,1)} %collective-permute-done), kind=kLoop, calls=%fused_computation.19 | loop fusion | flops 25165824 | bytes 50331648 | tf_op jit(solution)/shard_map/concatenate | solution.py:29
  165.4 911.6 %while.14 = (s32[]{:T(128)}, f32[16,2048,128]{2,1,0:T(8,128)}, s32[16]{0:T(128)S(1)}, s32[16,16]{0,1:T(8,128)S(1)}, bf16[32,2048,256]{2,1,0:T(8,128)(2,1)}, /*in...) while((s32[]{:T(128)}, f32[16,2048,128]{2,1,0:T(8,128)}, ...), condition=%wide.region_3.4_spmd.clone, body=%wide.region_2.3_spmd.clone.sunk | while | flops 2172651776 | bytes 142615312 | solution.py:49
  242.7 14.5 %fusion.27 = f32[16,8,256,128]{3,2,1,0:T(8,128)} fusion(bf16[16,8,256,256]{3,2,1,0:T(8,128)(2,1)} %bitcast.30, pred[16]{0:T(512)(128)(4,1)S(1)} %get-tuple-element.238, bf16[16,8,256,128]{3,2,1,0:T(8,128)(2,1)} %bitcast.31, pred[16]{0:T(512)(128)(4,1)S(1)} %get-tuple-element.240), kind=kOutput, calls=%fused_computation.4.clone.1 | convolution fusion | flops 2160066560 | bytes 41943072 | tf_op jit(solution)/shard_map/while/body/eval_jaxpr/kbgc,kbct->kbgt/dot_general | solution.py:39
  257.1 17.8 %fusion.28 = f32[16,2048,128]{2,1,0:T(8,128)} fusion(f32[16,8,256,128]{3,2,1,0:T(8,128)} %fusion.27, f32[16,2048,128]{2,1,0:T(8,128)} %get-tuple-element.251, pred[16]{0:T(512)(128)(4,1)S(1)} %broadcast_compare_fusion.2, pred[]{:T(512)S(6)} %compare.7), kind=kLoop, calls=%fused_computation.3.clone.1 | loop fusion | flops 12582912 | bytes 50331664 | tf_op jit(solution)/shard_map/while/body/eval_jaxpr/add | solution.py:46
  299.8 14.1 %fusion.27 = f32[16,8,256,128]{3,2,1,0:T(8,128)} fusion(bf16[16,8,256,256]{3,2,1,0:T(8,128)(2,1)} %bitcast.30, pred[16]{0:T(512)(128)(4,1)S(1)} %get-tuple-element.238, bf16[16,8,256,128]{3,2,1,0:T(8,128)(2,1)} %bitcast.31, pred[16]{0:T(512)(128)(4,1)S(1)} %get-tuple-element.240), kind=kOutput, calls=%fused_computation.4.clone.1 | convolution fusion | flops 2160066560 | bytes 41943072 | tf_op jit(solution)/shard_map/while/body/eval_jaxpr/kbgc,kbct->kbgt/dot_general | solution.py:39
  313.9 17.8 %fusion.28 = f32[16,2048,128]{2,1,0:T(8,128)} fusion(f32[16,8,256,128]{3,2,1,0:T(8,128)} %fusion.27, f32[16,2048,128]{2,1,0:T(8,128)} %get-tuple-element.251, pred[16]{0:T(512)(128)(4,1)S(1)} %broadcast_compare_fusion.2, pred[]{:T(512)S(6)} %compare.7), kind=kLoop, calls=%fused_computation.3.clone.1 | loop fusion | flops 12582912 | bytes 50331664 | tf_op jit(solution)/shard_map/while/body/eval_jaxpr/add | solution.py:46
  356.8 14.1 %fusion.27 = f32[16,8,256,128]{3,2,1,0:T(8,128)} fusion(bf16[16,8,256,256]{3,2,1,0:T(8,128)(2,1)} %bitcast.30, pred[16]{0:T(512)(128)(4,1)S(1)} %get-tuple-element.238, bf16[16,8,256,128]{3,2,1,0:T(8,128)(2,1)} %bitcast.31, pred[16]{0:T(512)(128)(4,1)S(1)} %get-tuple-element.240), kind=kOutput, calls=%fused_computation.4.clone.1 | convolution fusion | flops 2160066560 | bytes 41943072 | tf_op jit(solution)/shard_map/while/body/eval_jaxpr/kbgc,kbct->kbgt/dot_general | solution.py:39
  371.0 17.8 %fusion.28 = f32[16,2048,128]{2,1,0:T(8,128)} fusion(f32[16,8,256,128]{3,2,1,0:T(8,128)} %fusion.27, f32[16,2048,128]{2,1,0:T(8,128)} %get-tuple-element.251, pred[16]{0:T(512)(128)(4,1)S(1)} %broadcast_compare_fusion.2, pred[]{:T(512)S(6)} %compare.7), kind=kLoop, calls=%fused_computation.3.clone.1 | loop fusion | flops 12582912 | bytes 50331664 | tf_op jit(solution)/shard_map/while/body/eval_jaxpr/add | solution.py:46
  413.7 14.1 %fusion.27 = f32[16,8,256,128]{3,2,1,0:T(8,128)} fusion(bf16[16,8,256,256]{3,2,1,0:T(8,128)(2,1)} %bitcast.30, pred[16]{0:T(512)(128)(4,1)S(1)} %get-tuple-element.238, bf16[16,8,256,128]{3,2,1,0:T(8,128)(2,1)} %bitcast.31, pred[16]{0:T(512)(128)(4,1)S(1)} %get-tuple-element.240), kind=kOutput, calls=%fused_computation.4.clone.1 | convolution fusion | flops 2160066560 | bytes 41943072 | tf_op jit(solution)/shard_map/while/body/eval_jaxpr/kbgc,kbct->kbgt/dot_general | solution.py:39
  427.8 17.8 %fusion.28 = f32[16,2048,128]{2,1,0:T(8,128)} fusion(f32[16,8,256,128]{3,2,1,0:T(8,128)} %fusion.27, f32[16,2048,128]{2,1,0:T(8,128)} %get-tuple-element.251, pred[16]{0:T(512)(128)(4,1)S(1)} %broadcast_compare_fusion.2, pred[]{:T(512)S(6)} %compare.7), kind=kLoop, calls=%fused_computation.3.clone.1 | loop fusion | flops 12582912 | bytes 50331664 | tf_op jit(solution)/shard_map/while/body/eval_jaxpr/add | solution.py:46
  470.5 14.1 %fusion.27 = f32[16,8,256,128]{3,2,1,0:T(8,128)} fusion(bf16[16,8,256,256]{3,2,1,0:T(8,128)(2,1)} %bitcast.30, pred[16]{0:T(512)(128)(4,1)S(1)} %get-tuple-element.238, bf16[16,8,256,128]{3,2,1,0:T(8,128)(2,1)} %bitcast.31, pred[16]{0:T(512)(128)(4,1)S(1)} %get-tuple-element.240), kind=kOutput, calls=%fused_computation.4.clone.1 | convolution fusion | flops 2160066560 | bytes 41943072 | tf_op jit(solution)/shard_map/while/body/eval_jaxpr/kbgc,kbct->kbgt/dot_general | solution.py:39
  484.6 17.8 %fusion.28 = f32[16,2048,128]{2,1,0:T(8,128)} fusion(f32[16,8,256,128]{3,2,1,0:T(8,128)} %fusion.27, f32[16,2048,128]{2,1,0:T(8,128)} %get-tuple-element.251, pred[16]{0:T(512)(128)(4,1)S(1)} %broadcast_compare_fusion.2, pred[]{:T(512)S(6)} %compare.7), kind=kLoop, calls=%fused_computation.3.clone.1 | loop fusion | flops 12582912 | bytes 50331664 | tf_op jit(solution)/shard_map/while/body/eval_jaxpr/add | solution.py:46
  527.4 14.1 %fusion.27 = f32[16,8,256,128]{3,2,1,0:T(8,128)} fusion(bf16[16,8,256,256]{3,2,1,0:T(8,128)(2,1)} %bitcast.30, pred[16]{0:T(512)(128)(4,1)S(1)} %get-tuple-element.238, bf16[16,8,256,128]{3,2,1,0:T(8,128)(2,1)} %bitcast.31, pred[16]{0:T(512)(128)(4,1)S(1)} %get-tuple-element.240), kind=kOutput, calls=%fused_computation.4.clone.1 | convolution fusion | flops 2160066560 | bytes 41943072 | tf_op jit(solution)/shard_map/while/body/eval_jaxpr/kbgc,kbct->kbgt/dot_general | solution.py:39
  541.5 17.8 %fusion.28 = f32[16,2048,128]{2,1,0:T(8,128)} fusion(f32[16,8,256,128]{3,2,1,0:T(8,128)} %fusion.27, f32[16,2048,128]{2,1,0:T(8,128)} %get-tuple-element.251, pred[16]{0:T(512)(128)(4,1)S(1)} %broadcast_compare_fusion.2, pred[]{:T(512)S(6)} %compare.7), kind=kLoop, calls=%fused_computation.3.clone.1 | loop fusion | flops 12582912 | bytes 50331664 | tf_op jit(solution)/shard_map/while/body/eval_jaxpr/add | solution.py:46
  584.9 14.1 %fusion.27 = f32[16,8,256,128]{3,2,1,0:T(8,128)} fusion(bf16[16,8,256,256]{3,2,1,0:T(8,128)(2,1)} %bitcast.30, pred[16]{0:T(512)(128)(4,1)S(1)} %get-tuple-element.238, bf16[16,8,256,128]{3,2,1,0:T(8,128)(2,1)} %bitcast.31, pred[16]{0:T(512)(128)(4,1)S(1)} %get-tuple-element.240), kind=kOutput, calls=%fused_computation.4.clone.1 | convolution fusion | flops 2160066560 | bytes 41943072 | tf_op jit(solution)/shard_map/while/body/eval_jaxpr/kbgc,kbct->kbgt/dot_general | solution.py:39
  599.0 17.8 %fusion.28 = f32[16,2048,128]{2,1,0:T(8,128)} fusion(f32[16,8,256,128]{3,2,1,0:T(8,128)} %fusion.27, f32[16,2048,128]{2,1,0:T(8,128)} %get-tuple-element.251, pred[16]{0:T(512)(128)(4,1)S(1)} %broadcast_compare_fusion.2, pred[]{:T(512)S(6)} %compare.7), kind=kLoop, calls=%fused_computation.3.clone.1 | loop fusion | flops 12582912 | bytes 50331664 | tf_op jit(solution)/shard_map/while/body/eval_jaxpr/add | solution.py:46
  655.8 17.8 %fusion.28 = f32[16,2048,128]{2,1,0:T(8,128)} fusion(f32[16,8,256,128]{3,2,1,0:T(8,128)} %fusion.27, f32[16,2048,128]{2,1,0:T(8,128)} %get-tuple-element.251, pred[16]{0:T(512)(128)(4,1)S(1)} %broadcast_compare_fusion.2, pred[]{:T(512)S(6)} %compare.7), kind=kLoop, calls=%fused_computation.3.clone.1 | loop fusion | flops 12582912 | bytes 50331664 | tf_op jit(solution)/shard_map/while/body/eval_jaxpr/add | solution.py:46
  698.5 14.1 %fusion.27 = f32[16,8,256,128]{3,2,1,0:T(8,128)} fusion(bf16[16,8,256,256]{3,2,1,0:T(8,128)(2,1)} %bitcast.30, pred[16]{0:T(512)(128)(4,1)S(1)} %get-tuple-element.238, bf16[16,8,256,128]{3,2,1,0:T(8,128)(2,1)} %bitcast.31, pred[16]{0:T(512)(128)(4,1)S(1)} %get-tuple-element.240), kind=kOutput, calls=%fused_computation.4.clone.1 | convolution fusion | flops 2160066560 | bytes 41943072 | tf_op jit(solution)/shard_map/while/body/eval_jaxpr/kbgc,kbct->kbgt/dot_general | solution.py:39
  712.6 17.8 %fusion.28 = f32[16,2048,128]{2,1,0:T(8,128)} fusion(f32[16,8,256,128]{3,2,1,0:T(8,128)} %fusion.27, f32[16,2048,128]{2,1,0:T(8,128)} %get-tuple-element.251, pred[16]{0:T(512)(128)(4,1)S(1)} %broadcast_compare_fusion.2, pred[]{:T(512)S(6)} %compare.7), kind=kLoop, calls=%fused_computation.3.clone.1 | loop fusion | flops 12582912 | bytes 50331664 | tf_op jit(solution)/shard_map/while/body/eval_jaxpr/add | solution.py:46
  755.3 14.1 %fusion.27 = f32[16,8,256,128]{3,2,1,0:T(8,128)} fusion(bf16[16,8,256,256]{3,2,1,0:T(8,128)(2,1)} %bitcast.30, pred[16]{0:T(512)(128)(4,1)S(1)} %get-tuple-element.238, bf16[16,8,256,128]{3,2,1,0:T(8,128)(2,1)} %bitcast.31, pred[16]{0:T(512)(128)(4,1)S(1)} %get-tuple-element.240), kind=kOutput, calls=%fused_computation.4.clone.1 | convolution fusion | flops 2160066560 | bytes 41943072 | tf_op jit(solution)/shard_map/while/body/eval_jaxpr/kbgc,kbct->kbgt/dot_general | solution.py:39
  769.4 17.8 %fusion.28 = f32[16,2048,128]{2,1,0:T(8,128)} fusion(f32[16,8,256,128]{3,2,1,0:T(8,128)} %fusion.27, f32[16,2048,128]{2,1,0:T(8,128)} %get-tuple-element.251, pred[16]{0:T(512)(128)(4,1)S(1)} %broadcast_compare_fusion.2, pred[]{:T(512)S(6)} %compare.7), kind=kLoop, calls=%fused_computation.3.clone.1 | loop fusion | flops 12582912 | bytes 50331664 | tf_op jit(solution)/shard_map/while/body/eval_jaxpr/add | solution.py:46
  813.8 14.1 %fusion.27 = f32[16,8,256,128]{3,2,1,0:T(8,128)} fusion(bf16[16,8,256,256]{3,2,1,0:T(8,128)(2,1)} %bitcast.30, pred[16]{0:T(512)(128)(4,1)S(1)} %get-tuple-element.238, bf16[16,8,256,128]{3,2,1,0:T(8,128)(2,1)} %bitcast.31, pred[16]{0:T(512)(128)(4,1)S(1)} %get-tuple-element.240), kind=kOutput, calls=%fused_computation.4.clone.1 | convolution fusion | flops 2160066560 | bytes 41943072 | tf_op jit(solution)/shard_map/while/body/eval_jaxpr/kbgc,kbct->kbgt/dot_general | solution.py:39
  828.0 17.8 %fusion.28 = f32[16,2048,128]{2,1,0:T(8,128)} fusion(f32[16,8,256,128]{3,2,1,0:T(8,128)} %fusion.27, f32[16,2048,128]{2,1,0:T(8,128)} %get-tuple-element.251, pred[16]{0:T(512)(128)(4,1)S(1)} %broadcast_compare_fusion.2, pred[]{:T(512)S(6)} %compare.7), kind=kLoop, calls=%fused_computation.3.clone.1 | loop fusion | flops 12582912 | bytes 50331664 | tf_op jit(solution)/shard_map/while/body/eval_jaxpr/add | solution.py:46
  886.4 17.8 %fusion.28 = f32[16,2048,128]{2,1,0:T(8,128)} fusion(f32[16,8,256,128]{3,2,1,0:T(8,128)} %fusion.27, f32[16,2048,128]{2,1,0:T(8,128)} %get-tuple-element.251, pred[16]{0:T(512)(128)(4,1)S(1)} %broadcast_compare_fusion.2, pred[]{:T(512)S(6)} %compare.7), kind=kLoop, calls=%fused_computation.3.clone.1 | loop fusion | flops 12582912 | bytes 50331664 | tf_op jit(solution)/shard_map/while/body/eval_jaxpr/add | solution.py:46
  929.5 14.1 %fusion.27 = f32[16,8,256,128]{3,2,1,0:T(8,128)} fusion(bf16[16,8,256,256]{3,2,1,0:T(8,128)(2,1)} %bitcast.30, pred[16]{0:T(512)(128)(4,1)S(1)} %get-tuple-element.238, bf16[16,8,256,128]{3,2,1,0:T(8,128)(2,1)} %bitcast.31, pred[16]{0:T(512)(128)(4,1)S(1)} %get-tuple-element.240), kind=kOutput, calls=%fused_computation.4.clone.1 | convolution fusion | flops 2160066560 | bytes 41943072 | tf_op jit(solution)/shard_map/while/body/eval_jaxpr/kbgc,kbct->kbgt/dot_general | solution.py:39
  943.6 17.8 %fusion.28 = f32[16,2048,128]{2,1,0:T(8,128)} fusion(f32[16,8,256,128]{3,2,1,0:T(8,128)} %fusion.27, f32[16,2048,128]{2,1,0:T(8,128)} %get-tuple-element.251, pred[16]{0:T(512)(128)(4,1)S(1)} %broadcast_compare_fusion.2, pred[]{:T(512)S(6)} %compare.7), kind=kLoop, calls=%fused_computation.3.clone.1 | loop fusion | flops 12582912 | bytes 50331664 | tf_op jit(solution)/shard_map/while/body/eval_jaxpr/add | solution.py:46
  987.3 14.1 %fusion.27 = f32[16,8,256,128]{3,2,1,0:T(8,128)} fusion(bf16[16,8,256,256]{3,2,1,0:T(8,128)(2,1)} %bitcast.30, pred[16]{0:T(512)(128)(4,1)S(1)} %get-tuple-element.238, bf16[16,8,256,128]{3,2,1,0:T(8,128)(2,1)} %bitcast.31, pred[16]{0:T(512)(128)(4,1)S(1)} %get-tuple-element.240), kind=kOutput, calls=%fused_computation.4.clone.1 | convolution fusion | flops 2160066560 | bytes 41943072 | tf_op jit(solution)/shard_map/while/body/eval_jaxpr/kbgc,kbct->kbgt/dot_general | solution.py:39
  1001.5 17.8 %fusion.28 = f32[16,2048,128]{2,1,0:T(8,128)} fusion(f32[16,8,256,128]{3,2,1,0:T(8,128)} %fusion.27, f32[16,2048,128]{2,1,0:T(8,128)} %get-tuple-element.251, pred[16]{0:T(512)(128)(4,1)S(1)} %broadcast_compare_fusion.2, pred[]{:T(512)S(6)} %compare.7), kind=kLoop, calls=%fused_computation.3.clone.1 | loop fusion | flops 12582912 | bytes 50331664 | tf_op jit(solution)/shard_map/while/body/eval_jaxpr/add | solution.py:46
  1045.1 14.1 %fusion.27 = f32[16,8,256,128]{3,2,1,0:T(8,128)} fusion(bf16[16,8,256,256]{3,2,1,0:T(8,128)(2,1)} %bitcast.30, pred[16]{0:T(512)(128)(4,1)S(1)} %get-tuple-element.238, bf16[16,8,256,128]{3,2,1,0:T(8,128)(2,1)} %bitcast.31, pred[16]{0:T(512)(128)(4,1)S(1)} %get-tuple-element.240), kind=kOutput, calls=%fused_computation.4.clone.1 | convolution fusion | flops 2160066560 | bytes 41943072 | tf_op jit(solution)/shard_map/while/body/eval_jaxpr/kbgc,kbct->kbgt/dot_general | solution.py:39
  1059.2 17.8 %fusion.28 = f32[16,2048,128]{2,1,0:T(8,128)} fusion(f32[16,8,256,128]{3,2,1,0:T(8,128)} %fusion.27, f32[16,2048,128]{2,1,0:T(8,128)} %get-tuple-element.251, pred[16]{0:T(512)(128)(4,1)S(1)} %broadcast_compare_fusion.2, pred[]{:T(512)S(6)} %compare.7), kind=kLoop, calls=%fused_computation.3.clone.1 | loop fusion | flops 12582912 | bytes 50331664 | tf_op jit(solution)/shard_map/while/body/eval_jaxpr/add | solution.py:46
  1094.1 125.5 %reduce-scatter.2.cloned.1.call-done = f32[16,32,128]{2,1,0:T(8,128)} async-done(((f32[16,64,128]{2,1,0:T(8,128)}), f32[16,32,128]{2,1,0:T(8,128)}) %reduce-scatter.2.cloned.1.call-update) | async-done | bytes 262160 | tf_op jit(solution)/shard_map/reduce_scatter | solution.py:56
  (126 shorter events, 495.2 us)
Async XLA Ops:
  6.5 1087.5 %copy-start = (f32[16,64]{1,0:T(8,128)S(1)}, f32[16,64]{1,0:T(8,128)}, u32[]{:S(2)}) copy-start(f32[16,64]{1,0:T(8,128)} %param.12) | copy-start | bytes 12292
  6.5 1070.5 %all-gather.3.cloned.1.call-start = ((), (), s32[]{:S(2)}) async-start(), calls=%async_computation.2 | async-start | bytes 17825792 | tf_op jit(solution)/shard_map/all_gather | solution.py:31
  16.1 130.8 %collective-permute-start = (bf16[16,2048,128]{2,1,0:T(8,128)(2,1)}, bf16[16,2048,128]{2,1,0:T(8,128)(2,1)}, u32[]{:S(2)}, u32[]{:S(2)}) collective-permute-start(bf16[16,2048,128]{2,1,0:T(8,128)(2,1)} %get-tuple-element.189), channel_id=1, source_target_pairs={{0,2},{2,4},{4,6},{6,8},{8,10},{10,12},{12,14},{14,16},{16,18},{18... | collective-permute-start | bytes 25165832 | tf_op jit(solution)/shard_map/ppermute | solution.py:10
  16.6 130.3 %collective-permute-start.1 = (bf16[16,2048,128]{2,1,0:T(8,128)(2,1)}, bf16[16,2048,128]{2,1,0:T(8,128)(2,1)}, u32[]{:S(2)}, u32[]{:S(2)}) collective-permute-start(bf16[16,2048,128]{2,1,0:T(8,128)(2,1)} %get-tuple-element.189), channel_id=1, source_target_pairs={{0,30},{2,0},{4,2},{6,4},{8,6},{10,8},{12,10},{14,12},{16,14},{18,... | collective-permute-start | bytes 25165832 | tf_op jit(solution)/shard_map/ppermute | solution.py:10
  21.6 1198.1 %reduce-scatter.2.cloned.1.call-start = ((), (), s32[]{:S(2)}) async-start(), calls=%async_computation.1 | async-start | bytes 786432 | tf_op jit(solution)/shard_map/reduce_scatter | solution.py:56
  23.2 142.2 %copy-start.3 = (s32[16]{0:T(128)S(1)}, s32[16]{0:T(128)}, u32[]{:S(2)}) copy-start(s32[16]{0:T(128)} %param.16) | copy-start | bytes 196
  1077.1 6.7 copy-start.2
  1083.8 135.9 %copy-start.1 = (bf16[16,64,128]{2,1,0:T(8,128)(2,1)S(1)}, bf16[16,64,128]{2,1,0:T(8,128)(2,1)}, u32[]{:S(2)}) copy-start(bf16[16,64,128]{2,1,0:T(8,128)(2,1)} %param.11) | copy-start | bytes 786436
Sparse Core Ops, SparseCore 0:
  21.7 229.0 all-gather.2
  1094.1 125.4 reduce-scatter.1
